TPU v7x, 128 devices: a whole 4x4x4 slice. The times are simulated.
128 devices in a mesh: row: 16 (over y, x), col: 8 (over z, core).
Axes of the slice: x: 4, y: 4, z: 4, core: 2. Of those that a mesh axis runs over, the one named last changes fastest.
Arguments:
- amplitudes: bfloat16 [16384, 3072], P(('row', 'col')), may hold values from -6 to 6
- integrals: bfloat16 [8, 3072, 9600], P('col', None, 'row'), may hold values from -0.109375 to 0.109375
- irreps: int32 [16384], P(('row', 'col')), may hold values from 0 to 7, as said below
- row_mirror: int32 [16384], P(('row', 'col')), may hold values from 0 to 127, as said below
- col_mirror: int32 [9600], replicated, may hold values from 0 to 9599, as said below
Outputs:
- symmetrized: bfloat16 [16384, 9600], P(('row', 'col'))
Inputs may be any that keep to these rules, and one draw needn't show every extreme that they name: `irreps`: among the 128 pairs of one block, no irrep occurs more than 32 times; in every block one irrep, the same for all blocks, occurs exactly 32 times. A pair and its mirrored partner have the same irrep. `row_mirror`: within each block of 128 pairs the map is an involution without fixed points. `col_mirror`: an involution of the 9600 slab columns without fixed points.
All inputs are finite; a program needn't handle non-finite values.
Results may differ from a plain program's by a relative error of at most 0.0051.
Values may be sent and summed in bfloat16 or wider, within the bound.
A program may use at most 192 MiB of HBM per device.

v0:
```python
import jax
import jax.numpy as jnp
from jax import lax
from jax.sharding import PartitionSpec as P

IRREPS = 8


def body(amplitudes, integrals, irreps, row_mirror, col_mirror):
    pair_count = amplitudes.shape[0]
    contract = amplitudes.shape[1]
    col_count = lax.axis_size("col")
    per_owner = integrals.shape[0]
    capacity = pair_count // 4
    onehot = (irreps[:, None] == jnp.arange(IRREPS, dtype=jnp.int32)[None, :]).astype(jnp.int32)
    before = jnp.cumsum(onehot, axis=0) - onehot
    slot_index = jnp.sum(before * onehot, axis=1)
    owner_col = irreps // per_owner
    within = irreps % per_owner
    position = within * (col_count * capacity) + owner_col * capacity + slot_index
    outgoing = (
        jnp.zeros((per_owner * col_count * capacity, contract), jnp.bfloat16)
        .at[position]
        .set(amplitudes)
    )
    outgoing = outgoing.reshape(per_owner, col_count, capacity, contract)
    arrived = lax.all_to_all(outgoing, "col", split_axis=1, concat_axis=1, tiled=True)
    arrived = arrived.reshape(per_owner, col_count * capacity, contract)
    shares = jnp.einsum(
        "irk,iks->irs",
        lax.all_gather(arrived, "row", axis=1, tiled=True),
        integrals,
        preferred_element_type=jnp.float32,
    ).astype(jnp.bfloat16)
    result = lax.all_to_all(shares, "row", split_axis=1, concat_axis=2, tiled=True)
    slab_width = result.shape[2]
    result = result.reshape(per_owner, col_count, capacity, slab_width)
    returned = lax.all_to_all(result, "col", split_axis=1, concat_axis=1, tiled=True)
    ladder = returned.reshape(per_owner * col_count * capacity, slab_width)[position]
    mirrored = ladder[row_mirror][:, col_mirror]
    return (ladder.astype(jnp.float32) + mirrored.astype(jnp.float32)).astype(jnp.bfloat16)


def solution(mesh):
    return jax.shard_map(
        body,
        mesh=mesh,
        in_specs=(
            P(("row", "col"), None),
            P("col", None, "row"),
            P(("row", "col")),
            P(("row", "col")),
            P(),
        ),
        out_specs=P(("row", "col"), None),
        check_vma=False,
    )
```

profile of v0, /device:TPU:1, one launch (start us, length us, event | category | flops | bytes accessed | tf_op | source)
XLA Modules:
  0.0 593.4 jit_solution(5129053764023563648)
XLA Ops:
  6.5 0.0 all-gather.2.cloned.1.call-start
  6.5 0.7 fusion.12
  7.3 0.2 reduce_window_sum.11
  7.5 0.8 select_reduce_fusion
  8.3 0.7 compare_select_fusion.2
  9.0 2.8 scatter_custom_fusion
  11.8 27.5 %all_to_all.25 = bf16[1,8,32,3072]{3,2,0,1:T(8,128)(2,1)} all-to-all(bf16[1,8,32,3072]{3,2,0,1:T(8,128)(2,1)S(1)} %bitcast.34), channel_id=1, replica_groups=mesh['row'=16,'col'=8] {'col'}, dimensions={1} | all-to-all | bytes 3145728 | tf_op jit(solution)/shard_map/all_to_all | solution.py:27
  39.3 0.0 all-gather.2.cloned.1.call-update
  39.3 154.1 %all-gather.2.cloned.1.call-done = bf16[1,4096,3072]{2,1,0:T(8,128)(2,1)} async-done(((bf16[1,256,3072]{2,1,0:T(8,128)(2,1)}), bf16[1,4096,3072]{2,1,0:T(8,128)(2,1)}) %all-gather.2.cloned.1.call-update) | async-done | bytes 25165840 | tf_op jit(solution)/shard_map/all_gather | solution.py:31
  193.4 22.7 %fusion.5 = bf16[1,4096,600]{1,2,0:T(8,128)(2,1)} fusion(bf16[1,4096,3072]{2,1,0:T(8,128)(2,1)} %all-gather.2.cloned.1.call-done, bf16[1,3072,600]{1,2,0:T(8,128)(2,1)} %param.6), kind=kOutput, calls=%fused_computation.7 | convolution fusion | flops 15101952000 | bytes 33767424 | tf_op jit(solution)/shard_map/irk,iks->irs/dot_general | solution.py:29
  216.0 21.3 %copy.18 = bf16[1,4096,600]{2,0,1:T(2,128)(2,1)} copy(bf16[1,4096,600]{1,2,0:T(8,128)(2,1)} %fusion.5) | data formatting | bytes 9830400 | tf_op jit(solution)/shard_map/convert_element_type | solution.py:34
  237.3 0.5 broadcast.43
  237.8 113.4 %reduce = bf16[4096,600]{1,0:T(8,128)(2,1)} reduce(bf16[4096,1,600]{2,1,0:T(2,128)(2,1)} %bitcast.28, bf16[]{:T(256)} %broadcast.43), dimensions={1}, to_apply=%bitcast.26.reduce_sub_computation | reduce | bytes 9830402
  351.2 14.9 %reshape.67 = bf16[16,2,76800]{2,1,0:T(2,128)(2,1)} reshape(bf16[4096,600]{1,0:T(8,128)(2,1)} %reduce) | data formatting | bytes 9830400
  366.1 62.8 %all_to_all.26 = bf16[16,2,76800]{2,1,0:T(2,128)(2,1)} all-to-all(bf16[16,2,76800]{2,1,0:T(2,128)(2,1)} %reshape.67), channel_id=1, replica_groups=mesh['row'=16,'col'=8] {'row'}, dimensions={0} | all-to-all | bytes 9830400 | tf_op jit(solution)/shard_map/all_to_all | solution.py:35
  428.9 16.1 %reshape.68 = bf16[4096,1,600]{2,1,0:T(2,128)(2,1)} reshape(bf16[16,2,76800]{2,1,0:T(2,128)(2,1)} %all_to_all.26) | data formatting | bytes 9830400
  445.0 7.2 %copy.25 = bf16[1,4096,600]{2,1,0:T(8,128)(2,1)} copy(bf16[1,4096,600]{2,0,1:T(2,128)(2,1)} %bitcast.29) | data formatting | bytes 9830400
  452.2 8.6 %copy.24 = bf16[1,16,256,600]{2,1,3,0:T(8,128)(2,1)} copy(bf16[1,16,256,600]{3,2,1,0:T(8,128)(2,1)} %bitcast.30) | data formatting | bytes 9830400 | tf_op jit(solution)/shard_map/all_to_all | solution.py:35
  460.8 9.5 %copy.20 = bf16[1,256,16,600]{3,2,1,0:T(8,128)(2,1)} copy(bf16[1,256,16,600]{1,2,3,0:T(8,128)(2,1)} %bitcast.32) | data formatting | bytes 9830400 | tf_op jit(solution)/shard_map/all_to_all | solution.py:35
  470.3 9.1 %reshape.26 = bf16[1,8,32,9600]{3,2,1,0:T(8,128)(2,1)} reshape(bf16[1,256,16,600]{3,2,1,0:T(8,128)(2,1)} %copy.20) | data formatting | bytes 9830400 | tf_op jit(solution)/shard_map/reshape | solution.py:37
  479.4 0.0 copy-start.1
  479.4 0.0 copy-start
  479.4 6.4 %all-to-all-start.2 = ((bf16[1,8,32,9600]{3,2,0,1:T(8,128)(2,1)}), bf16[1,8,32,9600]{3,2,0,1:T(8,128)(2,1)}, u32[]{:S(2)}, u32[]{:S(2)}) async-start(bf16[1,8,32,9600]{3,2,0,1:T(8,128)(2,1)} %bitcast.31), calls=%async_computation.2 | async-start | bytes 9830400 | tf_op jit(solution)/shard_map/all_to_all | solution.py:38
  485.8 0.0 copy-done.1
  485.9 0.0 copy-done
  485.9 56.6 %all-to-all-done.2 = bf16[1,8,32,9600]{3,2,0,1:T(8,128)(2,1)} async-done(((bf16[1,8,32,9600]{3,2,0,1:T(8,128)(2,1)}), bf16[1,8,32,9600]{3,2,0,1:T(8,128)(2,1)}, u32[]{:S(2)}, u32[]{:S(2)}) %all-to-all-start.2) | async-done | bytes 4915232 | tf_op jit(solution)/shard_map/all_to_all | solution.py:38
  542.5 7.5 %gather_fusion = bf16[128,9600]{1,0:T(8,128)(2,1)S(1)} fusion(bf16[256,9600]{1,0:T(8,128)(2,1)} %bitcast.8, s32[1024]{0:T(1024)S(1)} %pad_clamp_fusion.2), kind=kCustom, calls=%fused_computation | custom fusion | bytes 4915712 | tf_op jit(solution)/shard_map/gather | solution.py:39
  550.0 3.5 gather_fusion.1
  553.5 4.3 copy.22
  557.9 20.7 %gather_fusion.2 = bf16[9600,128]{1,0:T(8,128)(2,1)} fusion(bf16[128,9600]{0,1:T(8,128)(2,1)} %copy.22, s32[10240]{0:T(1024)S(1)} %pad_clamp_fusion), kind=kCustom, calls=%fused_computation.2 | custom fusion | bytes 4953600 | tf_op jit(solution)/shard_map/gather | solution.py:40
  578.5 4.4 copy.23
  582.9 3.7 fusion.8
  (5 shorter events, 0.0 us)
Async XLA Ops:
  6.5 186.8 %all-gather.2.cloned.1.call-start = ((), (), s32[]{:S(2)}) async-start(), calls=%async_computation.3 | async-start | bytes 26738688 | tf_op jit(solution)/shard_map/all_gather | solution.py:31
  479.4 6.5 %copy-start.1 = (s32[128]{0:T(128)S(1)}, s32[128]{0:T(128)}, u32[]{:S(2)}) copy-start(s32[128]{0:T(128)} %param.8) | copy-start | bytes 1540
  479.4 6.5 %copy-start = (s32[9600]{0:T(1024)S(1)}, s32[9600]{0:T(1024)}, u32[]{:S(2)}) copy-start(s32[9600]{0:T(1024)} %param.9) | copy-start | bytes 115204
  479.4 63.1 %all-to-all-start.2 = ((bf16[1,8,32,9600]{3,2,0,1:T(8,128)(2,1)}), bf16[1,8,32,9600]{3,2,0,1:T(8,128)(2,1)}, u32[]{:S(2)}, u32[]{:S(2)}) async-start(bf16[1,8,32,9600]{3,2,0,1:T(8,128)(2,1)} %bitcast.31), calls=%async_computation.2 | async-start | bytes 9830400 | tf_op jit(solution)/shard_map/all_to_all | solution.py:38
Sparse Core Ops, SparseCore 0:
  39.4 153.9 all-gather.1
where the time goes:
time: 596 us; the launch traced here: 593 us
  waiting for transfers between devices  211 us (35%)
  local copies, waits for them, and re-layouts  130 us (22%)
  other arithmetic  119 us (20%)
  blocking collectives  90.3 us (15%)
  matrix products  22.7 us (4%)
  between operations  13.5 us (2%)
  starting transfers between devices  6.45 us (1%)
    all_gather x1, waiting for transfers between devices, body(): lax.all_gather(arrived, 'row', axis=1, tiled=True)  154 us
    unnamed x1, other arithmetic  113 us
    all_to_all x1, blocking collectives, body(): lax.all_to_all(shares, 'row', split_axis=1, concat_axis=2, tiled=True)  62.8 us
    all_to_all x1, waiting for transfers between devices, body(): lax.all_to_all(result, 'col', split_axis=1, concat_axis=1, tiled=True)  56.6 us
    unnamed x8, local copies, waits for them, and re-layouts  38.7 us
    gather x4, local copies, waits for them, and re-layouts, body(): mirrored = ladder[row_mirror][:, col_mirror]  32.9 us
    all_to_all x1, blocking collectives, body(): lax.all_to_all(outgoing, 'col', split_axis=1, concat_axis=1, tiled=True)  27.5 us
    dot_general x1, matrix products, body(): jnp.einsum('irk,iks->irs', lax.all_gather(arrived, 'row', axis=1, tiled=T...  22.7 us
  transfers between devices with their start and end apart: 2, of which 2 were waited for; matrix products, arithmetic and copies ran while one was open for 0% of the time, Pallas kernels for 0%

commit v1 on v0

--- a/solution.py
+++ b/solution.py
@@ -28,7 +28,9 @@
     arrived = arrived.reshape(per_owner, col_count * capacity, contract)
     shares = jnp.einsum(
         "irk,iks->irs",
-        lax.all_gather(arrived, "row", axis=1, tiled=True),
+        jnp.concatenate(
+            lax.all_to_all(jnp.stack([arrived] * lax.axis_size("row")), "row", 0, 0), axis=1
+        ),
         integrals,
         preferred_element_type=jnp.float32,
     ).astype(jnp.bfloat16)

time: 596 us -> 713 us (1.20)
  blocking collectives: 90.3 us -> 371 us
  waiting for transfers between devices: 211 us -> 56.6 us
  between operations: 13.5 us -> 0.11 us
    all_to_all x0 -> x1, blocking collectives: none -> 281 us  [body(): lax.all_to_all(jnp.stack([arrived] * lax.axis_size('row')), 'row', 0, 0)]
    all_gather x1 -> x0, waiting for transfers between devices: 154 us -> none  [body(): lax.all_gather(arrived, 'row', axis=1, tiled=True)]
    unnamed x8 -> x10, local copies, waits for them, and re-layouts: 38.7 us -> 38.7 us
  transfers between devices with their start and end apart: 2 -> 1, of which waited for: 2 -> 1; matrix products, arithmetic and copies ran while one was open for 0% -> 0% of each run, Pallas kernels for 0% -> 0%
where the time goes in v1:
time: 713 us; the launch traced here: 710 us
  blocking collectives  371 us (52%)
  local copies, waits for them, and re-layouts  134 us (19%)
  other arithmetic  119 us (17%)
  waiting for transfers between devices  56.6 us (8%)
  matrix products  21.6 us (3%)
  starting transfers between devices  7.79 us (1%)
    all_to_all x1, blocking collectives, body(): lax.all_to_all(jnp.stack([arrived] * lax.axis_size('row')), 'row', 0, 0)  281 us
    unnamed x1, other arithmetic  113 us
    all_to_all x1, blocking collectives, body(): lax.all_to_all(shares, 'row', split_axis=1, concat_axis=2, tiled=True)  62.3 us
    all_to_all x1, waiting for transfers between devices, body(): lax.all_to_all(result, 'col', split_axis=1, concat_axis=1, tiled=True)  56.6 us
    unnamed x10, local copies, waits for them, and re-layouts  38.7 us
    gather x4, local copies, waits for them, and re-layouts, body(): mirrored = ladder[row_mirror][:, col_mirror]  32.9 us
    all_to_all x1, blocking collectives, body(): lax.all_to_all(outgoing, 'col', split_axis=1, concat_axis=1, tiled=True)  27.4 us
    dot_general x1, matrix products, body(): jnp.einsum('irk,iks->irs', jnp.concatenate(lax.all_to_all(jnp.stack([arri...  21.6 us
  transfers between devices with their start and end apart: 1, of which 1 were waited for; matrix products, arithmetic and copies ran while one was open for 0% of the time, Pallas kernels for 0%

profile of v1, /device:TPU:1, one launch (start us, length us, event | category | flops | bytes accessed | tf_op | source)
XLA Modules:
  0.0 710.1 jit_solution(12568564353023716739)
XLA Ops:
  0.0 0.7 fusion.5
  0.7 0.2 reduce_window_sum.11
  0.9 0.8 select_reduce_fusion
  1.7 0.7 compare_select_fusion.2
  2.4 2.8 scatter_custom_fusion
  5.2 27.4 %all_to_all.30 = bf16[1,8,32,3072]{3,2,0,1:T(8,128)(2,1)S(1)} all-to-all(bf16[1,8,32,3072]{3,2,0,1:T(8,128)(2,1)S(1)} %bitcast.29), channel_id=1, replica_groups=mesh['row'=16,'col'=8] {'col'}, dimensions={1} | all-to-all | bytes 3145728 | tf_op jit(solution)/shard_map/all_to_all | solution.py:27
  32.6 3.2 stack.3
  35.8 0.0 copy-start.1
  35.8 281.2 %all_to_all.31 = bf16[16,1,256,3072]{3,2,1,0:T(8,128)(2,1)} all-to-all(bf16[16,1,256,3072]{3,2,1,0:T(8,128)(2,1)S(1)} %stack.3), channel_id=1, replica_groups=mesh['row'=16,'col'=8] {'row'}, dimensions={0} | all-to-all | bytes 50331648 | tf_op jit(solution)/shard_map/all_to_all | solution.py:32
  317.1 0.0 copy-done.1
  317.1 21.6 %fusion = bf16[1,4096,600]{1,2,0:T(8,128)(2,1)} fusion(bf16[4096,3072]{1,0:T(8,128)(2,1)} %bitcast.25, bf16[1,3072,600]{1,2,0:T(8,128)(2,1)S(1)} %copy-done.1), kind=kOutput, calls=%fused_computation.5 | convolution fusion | flops 15101952000 | bytes 33767424 | tf_op jit(solution)/shard_map/irk,iks->irs/dot_general | solution.py:29
  338.7 21.3 %copy.18 = bf16[1,4096,600]{2,0,1:T(2,128)(2,1)} copy(bf16[1,4096,600]{1,2,0:T(8,128)(2,1)} %fusion) | data formatting | bytes 9830400 | tf_op jit(solution)/shard_map/convert_element_type | solution.py:36
  360.0 0.5 broadcast.45
  360.5 113.4 %reduce = bf16[4096,600]{1,0:T(8,128)(2,1)} reduce(bf16[4096,1,600]{2,1,0:T(2,128)(2,1)} %bitcast.23, bf16[]{:T(256)} %broadcast.45), dimensions={1}, to_apply=%bitcast.20.reduce_sub_computation | reduce | bytes 9830402
  473.8 14.9 %reshape.69 = bf16[16,2,76800]{2,1,0:T(2,128)(2,1)} reshape(bf16[4096,600]{1,0:T(8,128)(2,1)} %reduce) | data formatting | bytes 9830400
  488.8 62.3 %all_to_all.32 = bf16[16,2,76800]{2,1,0:T(2,128)(2,1)} all-to-all(bf16[16,2,76800]{2,1,0:T(2,128)(2,1)} %reshape.69), channel_id=1, replica_groups=mesh['row'=16,'col'=8] {'row'}, dimensions={0} | all-to-all | bytes 9830400 | tf_op jit(solution)/shard_map/all_to_all | solution.py:37
  551.1 16.1 %reshape.70 = bf16[4096,1,600]{2,1,0:T(2,128)(2,1)} reshape(bf16[16,2,76800]{2,1,0:T(2,128)(2,1)} %all_to_all.32) | data formatting | bytes 9830400
  567.2 7.2 %copy.25 = bf16[1,4096,600]{2,1,0:T(8,128)(2,1)} copy(bf16[1,4096,600]{2,0,1:T(2,128)(2,1)} %bitcast.24) | data formatting | bytes 9830400
  574.4 8.6 %copy.24 = bf16[1,16,256,600]{2,1,3,0:T(8,128)(2,1)} copy(bf16[1,16,256,600]{3,2,1,0:T(8,128)(2,1)} %bitcast.26) | data formatting | bytes 9830400 | tf_op jit(solution)/shard_map/all_to_all | solution.py:37
  583.0 9.5 %copy.20 = bf16[1,256,16,600]{3,2,1,0:T(8,128)(2,1)} copy(bf16[1,256,16,600]{1,2,3,0:T(8,128)(2,1)} %bitcast.28) | data formatting | bytes 9830400 | tf_op jit(solution)/shard_map/all_to_all | solution.py:37
  592.5 9.1 %reshape.28 = bf16[1,8,32,9600]{3,2,1,0:T(8,128)(2,1)} reshape(bf16[1,256,16,600]{3,2,1,0:T(8,128)(2,1)} %copy.20) | data formatting | bytes 9830400 | tf_op jit(solution)/shard_map/reshape | solution.py:39
  601.6 0.0 copy-start.2
  601.6 0.0 copy-start
  601.6 7.8 %all-to-all-start.3 = ((bf16[1,8,32,9600]{3,2,0,1:T(8,128)(2,1)}), bf16[1,8,32,9600]{3,2,0,1:T(8,128)(2,1)}, u32[]{:S(2)}, u32[]{:S(2)}) async-start(bf16[1,8,32,9600]{3,2,0,1:T(8,128)(2,1)} %bitcast.27), calls=%async_computation.3 | async-start | bytes 9830400 | tf_op jit(solution)/shard_map/all_to_all | solution.py:40
  609.4 0.0 copy-done.2
  609.4 0.0 copy-done
  609.5 56.6 %all-to-all-done.3 = bf16[1,8,32,9600]{3,2,0,1:T(8,128)(2,1)} async-done(((bf16[1,8,32,9600]{3,2,0,1:T(8,128)(2,1)}), bf16[1,8,32,9600]{3,2,0,1:T(8,128)(2,1)}, u32[]{:S(2)}, u32[]{:S(2)}) %all-to-all-start.3) | async-done | bytes 4915232 | tf_op jit(solution)/shard_map/all_to_all | solution.py:40
  666.0 7.5 %gather_fusion = bf16[128,9600]{1,0:T(8,128)(2,1)S(1)} fusion(bf16[256,9600]{1,0:T(8,128)(2,1)} %bitcast.8, s32[1024]{0:T(1024)S(1)} %pad_clamp_fusion.2), kind=kCustom, calls=%fused_computation | custom fusion | bytes 4915712 | tf_op jit(solution)/shard_map/gather | solution.py:41
  673.5 3.5 gather_fusion.1
  677.1 4.3 copy.22
  681.4 20.7 %gather_fusion.2 = bf16[9600,128]{1,0:T(8,128)(2,1)} fusion(bf16[128,9600]{0,1:T(8,128)(2,1)} %copy.22, s32[10240]{0:T(1024)S(1)} %pad_clamp_fusion), kind=kCustom, calls=%fused_computation.2 | custom fusion | bytes 4953600 | tf_op jit(solution)/shard_map/gather | solution.py:42
  702.1 4.4 copy.23
  706.4 3.7 fusion.1
  (5 shorter events, 0.0 us)
Async XLA Ops:
  35.8 281.3 %copy-start.1 = (bf16[1,3072,600]{1,2,0:T(8,128)(2,1)S(1)}, bf16[1,3072,600]{1,2,0:T(8,128)(2,1)}, u32[]{:S(2)}) copy-start(bf16[1,3072,600]{1,2,0:T(8,128)(2,1)} %param.6) | copy-start | bytes 11059204
  601.6 7.8 %copy-start.2 = (s32[128]{0:T(128)S(1)}, s32[128]{0:T(128)}, u32[]{:S(2)}) copy-start(s32[128]{0:T(128)} %param.8) | copy-start | bytes 1540
  601.6 7.8 %copy-start = (s32[9600]{0:T(1024)S(1)}, s32[9600]{0:T(1024)}, u32[]{:S(2)}) copy-start(s32[9600]{0:T(1024)} %param.9) | copy-start | bytes 115204
  601.6 64.4 %all-to-all-start.3 = ((bf16[1,8,32,9600]{3,2,0,1:T(8,128)(2,1)}), bf16[1,8,32,9600]{3,2,0,1:T(8,128)(2,1)}, u32[]{:S(2)}, u32[]{:S(2)}) async-start(bf16[1,8,32,9600]{3,2,0,1:T(8,128)(2,1)} %bitcast.27), calls=%async_computation.3 | async-start | bytes 9830400 | tf_op jit(solution)/shard_map/all_to_all | solution.py:40
